TPU v7x, 256 devices: a whole 4x4x8 slice. The times are simulated.
256 devices in a mesh: row: 64 (over x, z, core), col: 4 (over y).
Axes of the slice: x: 4, y: 4, z: 8, core: 2. Of those that a mesh axis runs over, the one named last changes fastest.
Arguments:
- snapshots: float32 [131072, 4096], P('row', 'col'), may hold values from -1.5 to 1.5
- tests: float32 [2, 4096, 128], P(None, 'col'), may hold values from -0.09375 to 0.09375
Outputs:
- basis: float32 [131072, 256], P('row')
- coeffs: float32 [256, 4096], P(None, 'col')
All inputs are finite; a program needn't handle non-finite values.
Results may differ from a plain program's by a relative error of at most 0.0003.
Values sent between devices are 32-bit elements; how exact they have to be, the bound alone decides.
A program may use at most 128 MiB of HBM per device.

v0:
```python
import functools
import math

import jax
import jax.numpy as jnp
from jax import lax
from jax.experimental import pallas as pl
from jax.experimental.pallas import tpu as pltpu
from jax.sharding import PartitionSpec as P

F32 = jnp.float32
BF16 = jnp.bfloat16
XS, ZS, KS, YS = 4, 8, 2, 4
MESH = pl.DeviceIdType.MESH
ROWS = 2048
COLS = 1024
CH = 256
GROUP = XS * KS


def split(value):
    high = value.astype(BF16)
    low = (value - high.astype(F32)).astype(BF16)
    return high, low


def bdot(left, right):
    return jnp.dot(left, right, preferred_element_type=F32)


def dot3(left, right):
    (lh, ll), (rh, rl) = left, right
    return bdot(lh, rh) + (bdot(ll, rh) + bdot(lh, rl))


def fdot(left, right):
    return jnp.dot(left, right, precision=lax.Precision.HIGHEST, preferred_element_type=F32)


def ds(start, size):
    return pl.ds(pl.multiple_of(start, 8), size)


def comm_kernel(
    a_hbm, t_hbm, y_out, c_out, g_out,
    abuf, tbuf, ahi, alo, th, tl, ypart, rs, yfull,
    c2, cf, ccore, cx, cz, g2, gf, gg, gz, gy,
    load_sem, rs_send, rs_recv, ag_send, ag_recv,
    core_sem, x_send, x_recv, z_send, z_recv,
    gg_send, gg_recv, gz_send, gz_recv, gy_send, gy_recv, out_sem,
):
    r = lax.axis_index("row")
    c = lax.axis_index("col")
    x, z, k = r // (ZS * KS), (r // KS) % ZS, r % KS
    g = x * KS + k

    def row_of(xx, zz, kk):
        return xx * (ZS * KS) + zz * KS + kk

    def chunk(d, s):
        return lax.rem(c + (YS - 1 - s if d == 0 else 1 + s), YS)

    def base(d, j):
        return d * (YS * CH) + j * CH

    def remote(src, dst, ssem, rsem, **where):
        return pltpu.make_async_remote_copy(
            src_ref=src, dst_ref=dst, send_sem=ssem, recv_sem=rsem,
            device_id=where, device_id_type=MESH)

    loads = {}
    t_loads = [pltpu.make_async_copy(t_hbm.at[p], tbuf.at[p], load_sem.at[8 + p]) for p in range(2)]
    for copy in t_loads:
        copy.start()
    for s in range(YS):
        for d in range(2):
            rows = ds(base(d, chunk(d, s)), CH)
            loads[s, d] = pltpu.make_async_copy(a_hbm.at[rows], abuf.at[rows], load_sem.at[2 * s + d])
            loads[s, d].start()

    barrier = pltpu.get_barrier_semaphore()
    for o in range(1, YS):
        pl.semaphore_signal(barrier, inc=1, device_id={"col": lax.rem(c + o, YS)}, device_id_type=MESH)
    for o in range(1, GROUP):
        gp = lax.rem(g + o, GROUP)
        pl.semaphore_signal(barrier, inc=1, device_id={"row": row_of(gp // KS, z, gp % KS)}, device_id_type=MESH)
    for o in range(1, ZS):
        pl.semaphore_signal(barrier, inc=1, device_id={"row": row_of(x, lax.rem(z + o, ZS), k)}, device_id_type=MESH)

    for p in range(2):
        t_loads[p].wait()
        high, low = split(tbuf[p])
        th[:, p * 128:(p + 1) * 128] = high
        tl[:, p * 128:(p + 1) * 128] = low

    nexts = (lax.rem(c + 1, YS), lax.rem(c + YS - 1, YS))
    sends = []

    def rs_copy(p, d, s):
        src = ypart.at[p, ds(base(d, chunk(d, 0)), CH)] if s == 0 else rs.at[p, d, s - 1]
        return remote(src, rs.at[p, d, s], rs_send.at[p, d, s], rs_recv.at[p, d, s], col=nexts[d])

    def ag_copy(p, d, s):
        j = lax.rem(c + (YS - s if d == 0 else s), YS)
        ref = yfull.at[p, ds(base(d, j), CH)]
        return remote(ref, ref, ag_send.at[p, d, s], ag_recv.at[p, d, s], col=nexts[d])

    def sketch(d, s):
        loads[s, d].wait()
        rows = ds(base(d, chunk(d, s)), CH)
        high, low = split(abuf[rows, :])
        ahi[rows, :] = high
        alo[rows, :] = low
        part = dot3((high, low), (th[...], tl[...]))
        ypart[0, rows, :] = part[:, :128]
        ypart[1, rows, :] = part[:, 128:]

    for d in range(2):
        sketch(d, 0)
        if d == 0:
            pl.semaphore_wait(barrier, (YS - 1) + (GROUP - 1) + (ZS - 1))
        for p in range(2):
            copy = rs_copy(p, d, 0)
            copy.start()
            sends.append(copy)
    for d in range(2):
        sketch(d, 1)
    for s in range(1, YS):
        for p in range(2):
            for d in range(2):
                rs_copy(p, d, s - 1).wait_recv()
                rows = ds(base(d, chunk(d, s)), CH)
                if s < YS - 1:
                    rs[p, d, s - 1] = rs[p, d, s - 1] + ypart[p, rows, :]
                    copy = rs_copy(p, d, s)
                else:
                    yfull[p, rows, :] = rs[p, d, s - 1] + ypart[p, rows, :]
                    copy = ag_copy(p, d, 0)
                copy.start()
                sends.append(copy)
        if s < YS - 1:
            for d in range(2):
                sketch(d, s + 1)

    own = [jnp.concatenate([yfull[0, ds(base(d, c), CH), :], yfull[1, ds(base(d, c), CH), :]], axis=1) for d in range(2)]
    own = jnp.concatenate(own, axis=0)
    gram = dot3(split(own.T), split(own))
    g2[0:256, :] = gram[:, :128]
    g2[256:512, :] = gram[:, 128:]

    def g_copy(o):
        gp = lax.rem(g + o, GROUP)
        return remote(g2.at[ds(gp * 64, 64)], gg.at[o - 1], gg_send.at[0, o - 1], gg_recv.at[0, o - 1],
                      row=row_of(gp // KS, z, gp % KS))

    def gz_copy(o):
        zp = lax.rem(z + o, ZS)
        return remote(g2.at[ds(g * 64 + zp * 8, 8)], gz.at[o - 1], gz_send.at[0, o - 1], gz_recv.at[0, o - 1],
                      row=row_of(x, zp, k))

    gmine = ds(g * 64 + z * 8, 8)

    def gy_copy(o):
        return remote(g2.at[gmine], gy.at[o - 1], gy_send.at[o - 1], gy_recv.at[o - 1], col=lax.rem(c + o, YS))

    def gz_back(o):
        zp = lax.rem(z + o, ZS)
        return remote(gf.at[gmine], gf.at[gmine], gz_send.at[1, o - 1], gz_recv.at[1, o - 1], row=row_of(x, zp, k))

    def g_back(o):
        gp = lax.rem(g + o, GROUP)
        ref = gf.at[ds(g * 64, 64)]
        return remote(ref, ref, gg_send.at[1, o - 1], gg_recv.at[1, o - 1], row=row_of(gp // KS, z, gp % KS))

    def start(make, count):
        for o in range(1, count):
            copy = make(o)
            copy.start()
            sends.append(copy)

    def arrive(make, count):
        for o in range(1, count):
            make(o).wait_recv()

    def coeffs(d, j, first):
        rows = ds(base(d, j), CH)
        both = jnp.concatenate([yfull[0, rows, :].T, yfull[1, rows, :].T], axis=0)
        left = split(both)
        for t in range(4):
            lanes = slice(t * 256, (t + 1) * 256)
            part = dot3(left, (ahi[rows, lanes], alo[rows, lanes]))
            for h in range(2):
                out = slice((2 * t + h) * 256, (2 * t + h + 1) * 256)
                if first:
                    c2[out, :] = part[:, h * 128:(h + 1) * 128]
                else:
                    c2[out, :] += part[:, h * 128:(h + 1) * 128]

    start(g_copy, GROUP)
    coeffs(0, c, True)
    coeffs(1, c, False)

    def g_stage1():
        arrive(g_copy, GROUP)
        rows = ds(g * 64, 64)
        total = g2[rows, :]
        for o in range(GROUP - 1):
            total = total + gg[o]
        g2[rows, :] = total
        start(gz_copy, ZS)

    def g_stage2():
        arrive(gz_copy, ZS)
        total = g2[gmine, :]
        for o in range(ZS - 1):
            total = total + gz[o]
        g2[gmine, :] = total
        start(gy_copy, YS)

    def g_stage3():
        arrive(gy_copy, YS)
        gf[gmine, :] = (g2[gmine, :] + gy[1]) + (gy[0] + gy[2])
        start(gz_back, ZS)

    def g_stage4():
        arrive(gz_back, ZS)
        start(g_back, GROUP)

    stages = {0: g_stage1, 1: g_stage2, 2: g_stage3}
    for s in range(YS - 1):
        for p in range(2):
            for d in range(2):
                ag_copy(p, d, s).wait_recv()
                if s < YS - 2:
                    copy = ag_copy(p, d, s + 1)
                    copy.start()
                    sends.append(copy)
        stages[s]()
        for d in range(2):
            j = lax.rem(c + (YS - 1 - s if d == 0 else 1 + s), YS)
            coeffs(d, j, False)
    y_copy = pltpu.make_async_copy(yfull, y_out, out_sem.at[0])
    y_copy.start()

    half = k * 1024
    core_peer = row_of(x, z, 1 - k)
    core_copy = remote(c2.at[ds((1 - k) * 1024, 1024)], ccore, core_sem.at[0], core_sem.at[1], row=core_peer)
    core_copy.start()
    sends.append(core_copy)
    g_stage4()
    core_copy.wait_recv()
    mine = ds(half, 1024)
    c2[mine, :] += ccore[...]

    def x_copy(o):
        xp = lax.rem(x + o, XS)
        return remote(c2.at[ds(half + xp * 256, 256)], cx.at[o - 1], x_send.at[0, o - 1], x_recv.at[0, o - 1],
                      row=row_of(xp, z, k))

    quarter = half + x * 256

    def z_copy(o):
        zp = lax.rem(z + o, ZS)
        return remote(c2.at[ds(quarter + zp * 32, 32)], cz.at[o - 1], z_send.at[0, o - 1], z_recv.at[0, o - 1],
                      row=row_of(x, zp, k))

    piece = ds(quarter + z * 32, 32)

    def z_back(o):
        return remote(cf.at[piece], cf.at[piece], z_send.at[1, o - 1], z_recv.at[1, o - 1],
                      row=row_of(x, lax.rem(z + o, ZS), k))

    def x_back(o):
        ref = cf.at[ds(quarter, 256)]
        return remote(ref, ref, x_send.at[1, o - 1], x_recv.at[1, o - 1], row=row_of(lax.rem(x + o, XS), z, k))

    start(x_copy, XS)
    arrive(x_copy, XS)
    rows = ds(quarter, 256)
    c2[rows, :] = (c2[rows, :] + cx[0]) + (cx[1] + cx[2])
    start(z_copy, ZS)
    arrive(g_back, GROUP)
    g_out_copy = pltpu.make_async_copy(gf, g_out, out_sem.at[1])
    g_out_copy.start()
    arrive(z_copy, ZS)
    total = c2[piece, :]
    for o in range(ZS - 1):
        total = total + cz[o]
    cf[piece, :] = total
    start(z_back, ZS)
    arrive(z_back, ZS)
    start(x_back, XS)
    arrive(x_back, XS)
    core_back = remote(cf.at[mine], cf.at[mine], core_sem.at[2], core_sem.at[3], row=core_peer)
    core_back.start()
    sends.append(core_back)
    core_back.wait_recv()
    c_copy = pltpu.make_async_copy(cf, c_out, out_sem.at[2])
    c_copy.start()
    for copy in sends:
        copy.wait_send()
    y_copy.wait()
    g_out_copy.wait()
    c_copy.wait()


def eliminate(work):
    row = lax.broadcasted_iota(jnp.int32, (8, 256), 0)
    for b in range(16):
        slab = work[8 * b:8 * b + 8, :]
        for i in range(8):
            column = slab[:, 8 * b + i:8 * b + i + 1]
            scale = lax.rsqrt(column[i:i + 1, :])
            line = slab[i:i + 1, :] * scale
            below = slab - (column * scale) * line
            slab = jnp.where(row > i, below, jnp.where(row == i, jnp.broadcast_to(line, (8, 256)), slab))
        work[8 * b:8 * b + 8, :] = slab
        if b < 15:
            low = 8 * b + 8
            across = slab[:, :128].T
            work[low:, :] = work[low:, :] - fdot(across[low:, :], slab)


def finish_kernel(total, y_ref, c_ref, g_ref, basis_ref, coeff_ref, work):
    inv_total = 1.0 / total
    inv_root = 1.0 / math.sqrt(total)
    eye = (lax.broadcasted_iota(jnp.int32, (128, 128), 0) == lax.broadcasted_iota(jnp.int32, (128, 128), 1)).astype(F32)
    work[:, :128] = g_ref[0:128, :] * inv_total
    work[:, 128:] = eye
    eliminate(work)
    inv0 = work[:, 128:]
    cross = fdot(inv0, g_ref[256:384, :] * inv_total)
    work[:, :128] = g_ref[384:512, :] * inv_total - fdot(cross.T, cross)
    work[:, 128:] = eye
    eliminate(work)
    inv1 = work[:, 128:]
    corner = -fdot(fdot(inv1, cross.T), inv0)
    full = jnp.concatenate(
        [jnp.concatenate([inv0, jnp.zeros_like(inv0)], axis=1), jnp.concatenate([corner, inv1], axis=1)], axis=0)
    across = split(full.T)
    left = split(full)
    for i in range(8):
        rows = slice(i * 256, (i + 1) * 256)
        y = jnp.concatenate([y_ref[0, rows, :], y_ref[1, rows, :]], axis=1)
        basis_ref[rows, :] = dot3(split(y), across)
    for t in range(8):
        coeff_ref[:, t * 128:(t + 1) * 128] = dot3(left, split(c_ref[t * 256:(t + 1) * 256, :])) * inv_root


def per_device(snapshots, tests):
    total = ROWS * XS * ZS * KS
    vmem, dma = pltpu.VMEM, pltpu.SemaphoreType.DMA
    any_spec = pl.BlockSpec(memory_space=pl.ANY)
    y, cc, gg = pl.pallas_call(
        comm_kernel,
        out_shape=(
            jax.ShapeDtypeStruct((2, ROWS, 128), F32),
            jax.ShapeDtypeStruct((2048, 128), F32),
            jax.ShapeDtypeStruct((512, 128), F32)),
        in_specs=[any_spec, any_spec],
        out_specs=(any_spec, any_spec, any_spec),
        scratch_shapes=[
            vmem((ROWS, COLS), F32), vmem((2, COLS, 128), F32), vmem((ROWS, COLS), BF16), vmem((ROWS, COLS), BF16),
            vmem((COLS, 256), BF16), vmem((COLS, 256), BF16), vmem((2, ROWS, 128), F32),
            vmem((2, 2, 3, CH, 128), F32), vmem((2, ROWS, 128), F32),
            vmem((2048, 128), F32), vmem((2048, 128), F32), vmem((1024, 128), F32), vmem((3, 256, 128), F32),
            vmem((7, 32, 128), F32), vmem((512, 128), F32), vmem((512, 128), F32), vmem((7, 64, 128), F32),
            vmem((7, 8, 128), F32), vmem((3, 8, 128), F32),
            dma((10,)), dma((2, 2, 3)), dma((2, 2, 3)), dma((2, 2, 3)), dma((2, 2, 3)),
            dma((4,)), dma((2, 3)), dma((2, 3)), dma((2, 7)), dma((2, 7)),
            dma((2, 7)), dma((2, 7)), dma((2, 7)), dma((2, 7)), dma((3,)), dma((3,)), dma((3,))],
        compiler_params=pltpu.CompilerParams(collective_id=0, has_side_effects=True, vmem_limit_bytes=56 << 20),
    )(snapshots, tests)
    return pl.pallas_call(
        functools.partial(finish_kernel, float(total)),
        out_shape=(jax.ShapeDtypeStruct((ROWS, 256), F32), jax.ShapeDtypeStruct((256, COLS), F32)),
        scratch_shapes=[vmem((128, 256), F32)],
        compiler_params=pltpu.CompilerParams(vmem_limit_bytes=40 << 20),
    )(y, cc, gg)


def solution(mesh):
    in_specs = (P("row", "col"), P(None, "col", None))
    out_specs = (P("row", None), P(None, "col"))
    return jax.shard_map(per_device, mesh=mesh, in_specs=in_specs, out_specs=out_specs, check_vma=False)
```

profile of v0, /device:TPU:1, one launch (start us, length us, event | category | flops | bytes accessed | tf_op | source)
XLA Modules:
  0.0 119.1 jit_solution(259056863584679182)
XLA Ops:
  0.6 82.0 %shard_map.41 = (f32[2,2048,128]{2,1,0:T(8,128)}, f32[2048,128]{1,0:T(8,128)}, f32[512,128]{1,0:T(8,128)}) custom-call(f32[2048,1024]{1,0:T(8,128)} %a_hbm.1, f32[2,1024,128]{2,1,0:T(8,128)} %t_hbm.1), custom_call_target="tpu_custom_call" | custom-call | tf_op jit(solution)/shard_map/pallas_call | solution.py:354
  82.6 0.0 copy-start
  82.6 1.6 %copy-done = f32[2,2048,128]{2,1,0:T(8,128)S(1)} copy-done((f32[2,2048,128]{2,1,0:T(8,128)S(1)}, f32[2,2048,128]{2,1,0:T(8,128)}, u32[]{:S(2)}) %copy-start) | copy-done | bytes 2097176
  84.2 0.0 copy-start.1
  84.2 1.2 %copy-done.1 = f32[2048,128]{1,0:T(8,128)S(1)} copy-done((f32[2048,128]{1,0:T(8,128)S(1)}, f32[2048,128]{1,0:T(8,128)}, u32[]{:S(2)}) %copy-start.1) | copy-done | bytes 1048600
  85.4 0.0 copy-start.2
  85.4 0.9 copy-done.2
  86.4 32.8 %shard_map.42 = (f32[2048,256]{1,0:T(8,128)}, f32[256,1024]{1,0:T(8,128)}) custom-call(f32[2,2048,128]{2,1,0:T(8,128)S(1)} %copy-done, f32[2048,128]{1,0:T(8,128)S(1)} %copy-done.1, f32[512,128]{1,0:T(8,128)S(1)} %copy-done.2), custom_call_target="tpu_custom_call" | custom-call | tf_op jit(solution)/shard_map/pallas_call | solution.py:374
Async XLA Ops:
  82.6 1.6 %copy-start = (f32[2,2048,128]{2,1,0:T(8,128)S(1)}, f32[2,2048,128]{2,1,0:T(8,128)}, u32[]{:S(2)}) copy-start(f32[2,2048,128]{2,1,0:T(8,128)} %get-tuple-element.5.y_ref) | copy-start | bytes 6291460
  84.2 1.2 %copy-start.1 = (f32[2048,128]{1,0:T(8,128)S(1)}, f32[2048,128]{1,0:T(8,128)}, u32[]{:S(2)}) copy-start(f32[2048,128]{1,0:T(8,128)} %get-tuple-element.6.c_ref) | copy-start | bytes 3145732
  85.4 0.9 copy-start.2
where the time goes:
time: 119 us
  Pallas kernels  115 us (97%)
  local copies, waits for them, and re-layouts  3.76 us (3%)
    pallas_call x1, Pallas kernels, per_device(): pl.pallas_call(comm_kernel, out_shape=(jax.ShapeDtypeStruct((2, ROWS, 128...  82 us
    pallas_call x1, Pallas kernels, per_device(): pl.pallas_call(functools.partial(finish_kernel, float(total)), out_shape=...  32.8 us
    unnamed x6, local copies, waits for them, and re-layouts  3.76 us

commit v1 on v0

v1 whole, which is shorter than its diff:
```python
import math

import jax
import jax.numpy as jnp
from jax import lax
from jax.experimental import pallas as pl
from jax.experimental.pallas import tpu as pltpu
from jax.sharding import PartitionSpec as P

F32 = jnp.float32
BF16 = jnp.bfloat16
XS, ZS, KS, YS = 4, 8, 2, 4
MESH = pl.DeviceIdType.MESH
ROWS = 2048
COLS = 1024
CH = 256
GROUP = XS * KS
TOTAL = float(ROWS * XS * ZS * KS)
INV_TOTAL = 1.0 / TOTAL
INV_ROOT = 1.0 / math.sqrt(TOTAL)


def split(value):
    high = value.astype(BF16)
    low = (value - high.astype(F32)).astype(BF16)
    return high, low


def bdot(left, right):
    return jnp.dot(left, right, preferred_element_type=F32)


def dot3(left, right):
    (lh, ll), (rh, rl) = left, right
    return bdot(lh, rh) + (bdot(ll, rh) + bdot(lh, rl))


def fdot(left, right):
    return jnp.dot(left, right, precision=lax.Precision.HIGHEST, preferred_element_type=F32)


def ds(start, size):
    return pl.ds(pl.multiple_of(start, 8), size)


def twice(value):
    return jnp.concatenate([value, value], axis=1)


def eliminate(work, first):
    row = lax.broadcasted_iota(jnp.int32, (8, 256), 0)
    count = 4
    slabs = [work[8 * (first + q):8 * (first + q) + 8, :] for q in range(count)]
    for q in range(count):
        off = 8 * (first + q)

        def spread(slab, j):
            return jnp.broadcast_to(slab[:, off + j:off + j + 1], (8, 128))

        columns = [spread(slabs[q], j) for j in range(8)]
        diag = [[jnp.broadcast_to(columns[j][i:i + 1, :], (8, 128)) for j in range(i + 1)] for i in range(8)]
        lines = [jnp.broadcast_to(slabs[q][i:i + 1, :], (8, 256)) for i in range(8)]
        below = {p: [spread(slabs[p], j) for j in range(8)] for p in range(q + 1, count)}
        out = None
        for j in range(8):
            scale = lax.rsqrt(diag[j][j])
            lines[j] = lines[j] * twice(scale)
            low = [None] * (j + 1) + [diag[i][j] * scale for i in range(j + 1, 8)]
            for i in range(j + 1, 8):
                for m in range(j + 1, i + 1):
                    diag[i][m] = diag[i][m] - low[i] * low[m]
                lines[i] = lines[i] - twice(low[i]) * lines[j]
            for p in range(q + 1, count):
                factor = below[p][j] * scale
                for m in range(j + 1, 8):
                    below[p][m] = below[p][m] - factor * low[m]
                slabs[p] = slabs[p] - twice(factor) * lines[j]
            out = lines[j] if out is None else jnp.where(row == j, lines[j], out)
        slabs[q] = out
        work[off:off + 8, :] = out
    end = 8 * (first + count)
    if end < 128:
        done = work[8 * first:end, :]
        work[end:, :] = work[end:, :] - fdot(done[:, :128].T[end:, :], done)


def comm_kernel(
    a_hbm, t_hbm, basis_out, coeff_out,
    abuf, tbuf, ahi, alo, th, tl, ypart, rs, yfull,
    c2, cf, ccore, cx, cz, g2, gf, gg, gz, gy, work, inv, bbuf, obuf,
    load_sem, rs_send, rs_recv, ag_send, ag_recv,
    core_send, core_recv, x_send, x_recv, z_send, z_recv,
    gg_send, gg_recv, gz_send, gz_recv, gy_send, gy_recv, out_sem,
):
    r = lax.axis_index("row")
    c = lax.axis_index("col")
    x, z, k = r // (ZS * KS), (r // KS) % ZS, r % KS
    g = x * KS + k

    def row_of(xx, zz, kk):
        return xx * (ZS * KS) + zz * KS + kk

    def chunk(d, s):
        return lax.rem(c + (YS - 1 - s if d == 0 else 1 + s), YS)

    def base(d, j):
        return d * (YS * CH) + j * CH

    def remote(src, dst, ssem, rsem, **where):
        return pltpu.make_async_remote_copy(
            src_ref=src, dst_ref=dst, send_sem=ssem, recv_sem=rsem,
            device_id=where, device_id_type=MESH)

    sends = []

    def go(copy):
        copy.start()
        sends.append(copy)

    def start(make, count):
        for o in range(1, count):
            go(make(o))

    def arrive(make, count):
        for o in range(1, count):
            make(o).wait_recv()

    loads = {}
    t_loads = [pltpu.make_async_copy(t_hbm.at[p], tbuf.at[p], load_sem.at[8 + p]) for p in range(2)]
    for copy in t_loads:
        copy.start()
    for s in range(YS):
        for d in range(2):
            rows = ds(base(d, chunk(d, s)), CH)
            loads[s, d] = pltpu.make_async_copy(a_hbm.at[rows], abuf.at[rows], load_sem.at[2 * s + d])
            loads[s, d].start()

    barrier = pltpu.get_barrier_semaphore()
    for o in range(1, YS):
        pl.semaphore_signal(barrier, inc=1, device_id={"col": lax.rem(c + o, YS)}, device_id_type=MESH)
    for o in range(1, GROUP):
        gp = lax.rem(g + o, GROUP)
        pl.semaphore_signal(barrier, inc=1, device_id={"row": row_of(gp // KS, z, gp % KS)}, device_id_type=MESH)
    for o in range(1, ZS):
        pl.semaphore_signal(barrier, inc=1, device_id={"row": row_of(x, lax.rem(z + o, ZS), k)}, device_id_type=MESH)

    for p in range(2):
        t_loads[p].wait()
        high, low = split(tbuf[p])
        th[:, p * 128:(p + 1) * 128] = high
        tl[:, p * 128:(p + 1) * 128] = low

    nexts = (lax.rem(c + 1, YS), lax.rem(c + YS - 1, YS))

    def rs_copy(p, d, s):
        src = ypart.at[p, ds(base(d, chunk(d, 0)), CH)] if s == 0 else rs.at[p, d, s - 1]
        return remote(src, rs.at[p, d, s], rs_send.at[p, d, s], rs_recv.at[p, d, s], col=nexts[d])

    def ag_copy(p, d, s, h):
        j = lax.rem(c + (YS - s if d == 0 else s), YS)
        ref = yfull.at[p, ds(base(d, j) + h * (CH // 2), CH // 2)]
        return remote(ref, ref, ag_send.at[p, d, s, h], ag_recv.at[p, d, s, h], col=nexts[d])

    def sketch(d, s):
        loads[s, d].wait()
        rows = ds(base(d, chunk(d, s)), CH)
        high, low = split(abuf[rows, :])
        ahi[rows, :] = high
        alo[rows, :] = low
        part = dot3((high, low), (th[...], tl[...]))
        ypart[0, rows, :] = part[:, :128]
        ypart[1, rows, :] = part[:, 128:]

    def g_copy(o):
        gp = lax.rem(g + o, GROUP)
        return remote(g2.at[ds(gp * 64, 64)], gg.at[o - 1], gg_send.at[0, o - 1], gg_recv.at[0, o - 1],
                      row=row_of(gp // KS, z, gp % KS))

    def gz_copy(o):
        zp = lax.rem(z + o, ZS)
        return remote(g2.at[ds(g * 64 + zp * 8, 8)], gz.at[o - 1], gz_send.at[0, o - 1], gz_recv.at[0, o - 1],
                      row=row_of(x, zp, k))

    gmine = ds(g * 64 + z * 8, 8)

    def gy_copy(o):
        return remote(g2.at[gmine], gy.at[o - 1], gy_send.at[o - 1], gy_recv.at[o - 1], col=lax.rem(c + o, YS))

    def gz_back(o):
        return remote(gf.at[gmine], gf.at[gmine], gz_send.at[1, o - 1], gz_recv.at[1, o - 1],
                      row=row_of(x, lax.rem(z + o, ZS), k))

    def g_back(o):
        gp = lax.rem(g + o, GROUP)
        ref = gf.at[ds(g * 64, 64)]
        return remote(ref, ref, gg_send.at[1, o - 1], gg_recv.at[1, o - 1], row=row_of(gp // KS, z, gp % KS))

    def gram_local():
        own = [jnp.concatenate([yfull[p, ds(base(d, c), CH), :] for p in range(2)], axis=1) for d in range(2)]
        own = jnp.concatenate(own, axis=0)
        gram = dot3(split(own.T), split(own))
        g2[0:256, :] = gram[:, :128]
        g2[256:512, :] = gram[:, 128:]
        start(g_copy, GROUP)

    def g_stage1():
        arrive(g_copy, GROUP)
        rows = ds(g * 64, 64)
        total = g2[rows, :]
        for o in range(GROUP - 1):
            total = total + gg[o]
        g2[rows, :] = total
        start(gz_copy, ZS)

    def g_stage2():
        arrive(gz_copy, ZS)
        total = g2[gmine, :]
        for o in range(ZS - 1):
            total = total + gz[o]
        g2[gmine, :] = total
        start(gy_copy, YS)

    def g_stage3():
        arrive(gy_copy, YS)
        gf[gmine, :] = (g2[gmine, :] + gy[1]) + (gy[0] + gy[2])
        start(gz_back, ZS)

    def g_stage4():
        arrive(gz_back, ZS)
        start(g_back, GROUP)

    def g_stage5():
        arrive(g_back, GROUP)

    def product(p, d, j, first):
        rows = ds(base(d, j), CH)
        left = split(yfull[p, rows, :].T)
        for t in range(4):
            lanes = slice(t * 256, (t + 1) * 256)
            part = dot3(left, (ahi[rows, lanes], alo[rows, lanes]))
            for h in range(2):
                out = slice((2 * t + h) * 128, (2 * t + h + 1) * 128)
                if first:
                    c2[p, out, :] = part[:, h * 128:(h + 1) * 128]
                else:
                    c2[p, out, :] += part[:, h * 128:(h + 1) * 128]

    def step_products(p, s):
        for d in range(2):
            product(p, d, lax.rem(c + (YS - 1 - s if d == 0 else 1 + s), YS), False)

    half = k * 512
    mine = ds(half, 512)
    quarter = half + x * 128
    piece = ds(quarter + z * 16, 16)
    core_peer = row_of(x, z, 1 - k)

    def core_copy(p):
        return remote(c2.at[p, ds((1 - k) * 512, 512)], ccore.at[p], core_send.at[p, 0], core_recv.at[p, 0],
                      row=core_peer)

    def core_back(p):
        return remote(cf.at[p, mine], cf.at[p, mine], core_send.at[p, 1], core_recv.at[p, 1], row=core_peer)

    def x_copy(p):
        def make(o):
            xp = lax.rem(x + o, XS)
            return remote(c2.at[p, ds(half + xp * 128, 128)], cx.at[p, o - 1],
                          x_send.at[p, 0, o - 1], x_recv.at[p, 0, o - 1], row=row_of(xp, z, k))
        return make

    def z_copy(p):
        def make(o):
            zp = lax.rem(z + o, ZS)
            return remote(c2.at[p, ds(quarter + zp * 16, 16)], cz.at[p, o - 1],
                          z_send.at[p, 0, o - 1], z_recv.at[p, 0, o - 1], row=row_of(x, zp, k))
        return make

    def z_back(p):
        def make(o):
            return remote(cf.at[p, piece], cf.at[p, piece], z_send.at[p, 1, o - 1], z_recv.at[p, 1, o - 1],
                          row=row_of(x, lax.rem(z + o, ZS), k))
        return make

    def x_back(p):
        def make(o):
            ref = cf.at[p, ds(quarter, 128)]
            return remote(ref, ref, x_send.at[p, 1, o - 1], x_recv.at[p, 1, o - 1],
                          row=row_of(lax.rem(x + o, XS), z, k))
        return make

    def c_stage1(p):
        core_copy(p).wait_recv()
        c2[p, mine, :] += ccore[p]
        start(x_copy(p), XS)

    def c_stage2(p):
        arrive(x_copy(p), XS)
        rows = ds(quarter, 128)
        c2[p, rows, :] = (c2[p, rows, :] + cx[p, 0]) + (cx[p, 1] + cx[p, 2])
        start(z_copy(p), ZS)

    def c_stage3(p):
        arrive(z_copy(p), ZS)
        total = c2[p, piece, :]
        for o in range(ZS - 1):
            total = total + cz[p, o]
        cf[p, piece, :] = total
        start(z_back(p), ZS)

    def c_stage4(p):
        arrive(z_back(p), ZS)
        start(x_back(p), XS)

    def c_stage5(p):
        arrive(x_back(p), XS)
        go(core_back(p))

    def c_stage6(p):
        core_back(p).wait_recv()

    def eye():
        shape = (128, 128)
        same = lax.broadcasted_iota(jnp.int32, shape, 0) == lax.broadcasted_iota(jnp.int32, shape, 1)
        return same.astype(F32)

    def factor_start0():
        work[0, :, :128] = gf[0:128, :] * INV_TOTAL
        work[0, :, 128:] = eye()

    def factor_start1():
        cross = fdot(work[0, :, 128:], gf[256:384, :] * INV_TOTAL)
        work[1, :, :128] = gf[384:512, :] * INV_TOTAL - fdot(cross.T, cross)
        work[1, :, 128:] = eye()
        inv[:128, 128:] = cross

    def factor_end():
        inv0, inv1 = work[0, :, 128:], work[1, :, 128:]
        corner = -fdot(fdot(inv1, inv[:128, 128:].T), inv0)
        inv[:128, :128] = inv0
        inv[:128, 128:] = jnp.zeros_like(inv0)
        inv[128:, :128] = corner
        inv[128:, 128:] = inv1

    def gathered(p):
        return jnp.concatenate([cf[p, t * 128:(t + 1) * 128, :] for t in range(8)], axis=1)

    basis_copies = []

    def bases():
        across = split(inv[...].T)
        for i in range(8):
            rows = slice(i * CH, (i + 1) * CH)
            y = jnp.concatenate([yfull[0, rows, :], yfull[1, rows, :]], axis=1)
            bbuf[rows, :] = dot3(split(y), across)
            copy = pltpu.make_async_copy(bbuf.at[rows], basis_out.at[rows], out_sem.at[i])
            copy.start()
            basis_copies.append(copy)

    def ag_pass(p, s, h):
        for d in range(2):
            ag_copy(p, d, s, h).wait_recv()
            if s < YS - 2:
                go(ag_copy(p, d, s + 1, h))

    for d in range(2):
        sketch(d, 0)
        if d == 0:
            pl.semaphore_wait(barrier, (YS - 1) + (GROUP - 1) + (ZS - 1))
        for p in range(2):
            go(rs_copy(p, d, 0))
    for d in range(2):
        sketch(d, 1)
    for s in range(1, YS):
        for p in range(2):
            for d in range(2):
                rs_copy(p, d, s - 1).wait_recv()
                rows = ds(base(d, chunk(d, s)), CH)
                if s < YS - 1:
                    rs[p, d, s - 1] = rs[p, d, s - 1] + ypart[p, rows, :]
                    go(rs_copy(p, d, s))
                else:
                    yfull[p, rows, :] = rs[p, d, s - 1] + ypart[p, rows, :]
                    if p == 0:
                        for h in range(2):
                            go(ag_copy(0, d, 0, h))
        if s < YS - 1:
            for d in range(2):
                sketch(d, s + 1)

    gram_local()
    product(0, 0, c, True)
    product(0, 1, c, False)
    ag_pass(0, 0, 0)
    g_stage1()
    ag_pass(0, 0, 1)
    g_stage2()
    step_products(0, 0)
    ag_pass(0, 1, 0)
    g_stage3()
    ag_pass(0, 1, 1)
    for h in range(2):
        for d in range(2):
            go(ag_copy(1, d, 0, h))
    step_products(0, 1)
    g_stage4()
    ag_pass(0, 2, 0)
    ag_pass(0, 2, 1)
    step_products(0, 2)
    go(core_copy(0))
    g_stage5()
    factor_start0()
    eliminate(work.at[0], 0)
    c_stage1(0)
    ag_pass(1, 0, 0)
    product(1, 0, c, True)
    product(1, 1, c, False)
    ag_pass(1, 0, 1)
    eliminate(work.at[0], 4)
    eliminate(work.at[0], 8)
    step_products(1, 0)
    ag_pass(1, 1, 0)
    c_stage2(0)
    eliminate(work.at[0], 12)
    ag_pass(1, 1, 1)
    factor_start1()
    eliminate(work.at[1], 0)
    c_stage3(0)
    step_products(1, 1)
    ag_pass(1, 2, 0)
    ag_pass(1, 2, 1)
    step_products(1, 2)
    go(core_copy(1))
    c_stage4(0)
    eliminate(work.at[1], 4)
    c_stage1(1)
    eliminate(work.at[1], 8)
    eliminate(work.at[1], 12)
    c_stage5(0)
    c_stage2(1)
    factor_end()
    c_stage6(0)
    first = dot3(split(inv[:, :128]), split(gathered(0)))
    obuf[:128, :] = first[:128, :] * INV_ROOT
    obuf[128:, :] = first[128:, :]
    coeff_copy0 = pltpu.make_async_copy(obuf.at[0:128], coeff_out.at[0:128], out_sem.at[8])
    coeff_copy0.start()
    c_stage3(1)
    bases()
    c_stage4(1)
    c_stage5(1)
    c_stage6(1)
    last = dot3(split(inv[128:, 128:]), split(gathered(1)))
    obuf[128:, :] = (obuf[128:, :] + last) * INV_ROOT
    coeff_copy1 = pltpu.make_async_copy(obuf.at[128:256], coeff_out.at[128:256], out_sem.at[9])
    coeff_copy1.start()
    for copy in sends:
        copy.wait_send()
    for copy in basis_copies:
        copy.wait()
    coeff_copy0.wait()
    coeff_copy1.wait()


def per_device(snapshots, tests):
    vmem, dma = pltpu.VMEM, pltpu.SemaphoreType.DMA
    any_spec = pl.BlockSpec(memory_space=pl.ANY)
    return pl.pallas_call(
        comm_kernel,
        out_shape=(jax.ShapeDtypeStruct((ROWS, 256), F32), jax.ShapeDtypeStruct((256, COLS), F32)),
        in_specs=[any_spec, any_spec],
        out_specs=(any_spec, any_spec),
        scratch_shapes=[
            vmem((ROWS, COLS), F32), vmem((2, COLS, 128), F32), vmem((ROWS, COLS), BF16), vmem((ROWS, COLS), BF16),
            vmem((COLS, 256), BF16), vmem((COLS, 256), BF16), vmem((2, ROWS, 128), F32),
            vmem((2, 2, 3, CH, 128), F32), vmem((2, ROWS, 128), F32),
            vmem((2, 1024, 128), F32), vmem((2, 1024, 128), F32), vmem((2, 512, 128), F32),
            vmem((2, 3, 128, 128), F32), vmem((2, 7, 16, 128), F32),
            vmem((512, 128), F32), vmem((512, 128), F32), vmem((7, 64, 128), F32),
            vmem((7, 8, 128), F32), vmem((3, 8, 128), F32), vmem((2, 128, 256), F32), vmem((256, 256), F32),
            vmem((ROWS, 256), F32), vmem((256, COLS), F32),
            dma((10,)), dma((2, 2, 3)), dma((2, 2, 3)), dma((2, 2, 3, 2)), dma((2, 2, 3, 2)),
            dma((2, 2)), dma((2, 2)), dma((2, 2, 3)), dma((2, 2, 3)), dma((2, 2, 7)), dma((2, 2, 7)),
            dma((2, 7)), dma((2, 7)), dma((2, 7)), dma((2, 7)), dma((3,)), dma((3,)), dma((10,))],
        compiler_params=pltpu.CompilerParams(collective_id=0, has_side_effects=True, vmem_limit_bytes=56 << 20),
    )(snapshots, tests)


def solution(mesh):
    in_specs = (P("row", "col"), P(None, "col", None))
    out_specs = (P("row", None), P(None, "col"))
    return jax.shard_map(per_device, mesh=mesh, in_specs=in_specs, out_specs=out_specs, check_vma=False)
```

time: 119 us -> 104 us (0.87)
  Pallas kernels: 115 us -> 99.5 us
    pallas_call x2 -> x1, Pallas kernels: 115 us -> 99.5 us  [per_device(): pl.pallas_call(comm_kernel, out_shape=(jax.ShapeDtypeStruct((ROWS, 256),...]
    unnamed x6 -> x4, local copies, waits for them, and re-layouts: 3.76 us -> 4.11 us
where the time goes in v1:
time: 104 us
  Pallas kernels  99.5 us (96%)
  local copies, waits for them, and re-layouts  4.11 us (4%)
    pallas_call x1, Pallas kernels, per_device(): pl.pallas_call(comm_kernel, out_shape=(jax.ShapeDtypeStruct((ROWS, 256),...  99.5 us
    unnamed x4, local copies, waits for them, and re-layouts  4.11 us

profile of v1, /device:TPU:1, one launch (start us, length us, event | category | flops | bytes accessed | tf_op | source)
XLA Modules:
  0.0 104.2 jit_solution(12189379407600602010)
XLA Ops:
  0.6 99.5 %shard_map.41 = (f32[2048,256]{1,0:T(8,128)}, f32[256,1024]{1,0:T(8,128)}) custom-call(f32[2048,1024]{1,0:T(8,128)} %a_hbm.1, f32[2,1024,128]{2,1,0:T(8,128)} %t_hbm.1), custom_call_target="tpu_custom_call" | custom-call | tf_op jit(solution)/shard_map/pallas_call | solution.py:468
  100.1 0.0 copy-start
  100.1 3.1 %copy.6 = f32[2048,256]{1,0:T(8,128)} copy(f32[2048,256]{1,0:T(8,128)} %get-tuple-element.4) | data formatting | bytes 4194304
  103.2 0.0 copy-done
  103.2 1.0 copy.7
Async XLA Ops:
  100.1 3.1 %copy-start = (f32[256,1024]{1,0:T(8,128)S(1)}, f32[256,1024]{1,0:T(8,128)}, u32[]{:S(2)}) copy-start(f32[256,1024]{1,0:T(8,128)} %get-tuple-element.5) | copy-start | bytes 3145732

commit v2 on v1

--- a/solution.py
+++ b/solution.py
@@ -87,7 +87,7 @@
 def comm_kernel(
     a_hbm, t_hbm, basis_out, coeff_out,
     abuf, tbuf, ahi, alo, th, tl, ypart, rs, yfull,
-    c2, cf, ccore, cx, cz, g2, gf, gg, gz, gy, work, inv, bbuf, obuf,
+    c2, cf, ccore, cx, cz, g2, gf, gg, gz, gy, gt, work, inv, bbuf, obuf,
     load_sem, rs_send, rs_recv, ag_send, ag_recv,
     core_send, core_recv, x_send, x_recv, z_send, z_recv,
     gg_send, gg_recv, gz_send, gz_recv, gy_send, gy_recv, out_sem,
@@ -100,8 +100,8 @@
     def row_of(xx, zz, kk):
         return xx * (ZS * KS) + zz * KS + kk
 
-    def chunk(d, s):
-        return lax.rem(c + (YS - 1 - s if d == 0 else 1 + s), YS)
+    def chunk(step):
+        return lax.rem(c + step, YS)
 
     def base(d, j):
         return d * (YS * CH) + j * CH
@@ -125,45 +125,71 @@
         for o in range(1, count):
             make(o).wait_recv()
 
-    loads = {}
-    t_loads = [pltpu.make_async_copy(t_hbm.at[p], tbuf.at[p], load_sem.at[8 + p]) for p in range(2)]
-    for copy in t_loads:
-        copy.start()
-    for s in range(YS):
-        for d in range(2):
-            rows = ds(base(d, chunk(d, s)), CH)
-            loads[s, d] = pltpu.make_async_copy(a_hbm.at[rows], abuf.at[rows], load_sem.at[2 * s + d])
-            loads[s, d].start()
-
     barrier = pltpu.get_barrier_semaphore()
-    for o in range(1, YS):
-        pl.semaphore_signal(barrier, inc=1, device_id={"col": lax.rem(c + o, YS)}, device_id_type=MESH)
+    for o in range(1, ZS):
+        pl.semaphore_signal(barrier, inc=1, device_id={"row": row_of(x, lax.rem(z + o, ZS), k)}, device_id_type=MESH)
     for o in range(1, GROUP):
         gp = lax.rem(g + o, GROUP)
         pl.semaphore_signal(barrier, inc=1, device_id={"row": row_of(gp // KS, z, gp % KS)}, device_id_type=MESH)
-    for o in range(1, ZS):
-        pl.semaphore_signal(barrier, inc=1, device_id={"row": row_of(x, lax.rem(z + o, ZS), k)}, device_id_type=MESH)
-
+    for o in range(1, YS):
+        pl.semaphore_signal(barrier, inc=1, device_id={"col": chunk(o)}, device_id_type=MESH)
+
+    units = [(0, 2), (1, 2), (1, 1), (0, 3), (0, 1), (1, 3), (0, 0), (1, 0)]
+    t_loads = [pltpu.make_async_copy(t_hbm.at[p], tbuf.at[p], load_sem.at[8 + p]) for p in range(2)]
+    loads = {}
+    for i, (h, step) in enumerate(units):
+        rows = ds(base(h, chunk(step)), CH)
+        loads[h, step] = pltpu.make_async_copy(a_hbm.at[rows], abuf.at[rows], load_sem.at[i])
+    t_loads[0].start()
+    t_loads[1].start()
+    for unit in units:
+        loads[unit].start()
     for p in range(2):
         t_loads[p].wait()
         high, low = split(tbuf[p])
         th[:, p * 128:(p + 1) * 128] = high
         tl[:, p * 128:(p + 1) * 128] = low
 
-    nexts = (lax.rem(c + 1, YS), lax.rem(c + YS - 1, YS))
-
-    def rs_copy(p, d, s):
-        src = ypart.at[p, ds(base(d, chunk(d, 0)), CH)] if s == 0 else rs.at[p, d, s - 1]
-        return remote(src, rs.at[p, d, s], rs_send.at[p, d, s], rs_recv.at[p, d, s], col=nexts[d])
-
-    def ag_copy(p, d, s, h):
-        j = lax.rem(c + (YS - s if d == 0 else s), YS)
-        ref = yfull.at[p, ds(base(d, j) + h * (CH // 2), CH // 2)]
-        return remote(ref, ref, ag_send.at[p, d, s, h], ag_recv.at[p, d, s, h], col=nexts[d])
-
-    def sketch(d, s):
-        loads[s, d].wait()
-        rows = ds(base(d, chunk(d, s)), CH)
+    steps = (1, 3)
+
+    def to(d):
+        return chunk(steps[d])
+
+    def relay(p, d):
+        return remote(ypart.at[p, ds(base(d, chunk(2)), CH)], rs.at[p, d, 0],
+                      rs_send.at[p, d, 0], rs_recv.at[p, d, 0], col=to(d))
+
+    def direct(p, d):
+        return remote(ypart.at[p, ds(base(1 - d, to(d)), CH)], rs.at[p, d, 1],
+                      rs_send.at[p, d, 1], rs_recv.at[p, d, 1], col=to(d))
+
+    def relayed(p, d):
+        return remote(rs.at[p, d, 0], rs.at[p, d, 2], rs_send.at[p, d, 2], rs_recv.at[p, d, 2], col=to(d))
+
+    def pass_on(p):
+        for d in range(2):
+            relay(p, d).wait_recv()
+            rs[p, d, 0] = rs[p, d, 0] + ypart[p, ds(base(d, to(d)), CH), :]
+            go(relayed(p, d))
+
+    def own_sum(p):
+        for h in range(2):
+            direct(p, 1 - h).wait_recv()
+            relayed(p, h).wait_recv()
+            rows = ds(base(h, c), CH)
+            yfull[p, rows, :] = (rs[p, h, 2] + rs[p, 1 - h, 1]) + ypart[p, rows, :]
+
+    def gather(p, d, h):
+        ref = yfull.at[p, ds(base(h, c), CH)]
+        return remote(ref, ref, ag_send.at[p, d, h], ag_recv.at[p, d, h], col=to(d))
+
+    def gather_on(p, d):
+        ref = yfull.at[p, ds(base(d, to(1 - d)), CH)]
+        return remote(ref, ref, ag_send.at[p, d, 2], ag_recv.at[p, d, 2], col=to(d))
+
+    def sketch(h, step):
+        loads[h, step].wait()
+        rows = ds(base(h, chunk(step)), CH)
         high, low = split(abuf[rows, :])
         ahi[rows, :] = high
         alo[rows, :] = low
@@ -171,83 +197,92 @@
         ypart[0, rows, :] = part[:, :128]
         ypart[1, rows, :] = part[:, 128:]
 
-    def g_copy(o):
+    def g_rows(p, index):
+        return ds(index * (16 * (p + 1)), 16 * (p + 1))
+
+    def g_peer(o):
         gp = lax.rem(g + o, GROUP)
-        return remote(g2.at[ds(gp * 64, 64)], gg.at[o - 1], gg_send.at[0, o - 1], gg_recv.at[0, o - 1],
-                      row=row_of(gp // KS, z, gp % KS))
-
-    def gz_copy(o):
-        zp = lax.rem(z + o, ZS)
-        return remote(g2.at[ds(g * 64 + zp * 8, 8)], gz.at[o - 1], gz_send.at[0, o - 1], gz_recv.at[0, o - 1],
-                      row=row_of(x, zp, k))
-
-    gmine = ds(g * 64 + z * 8, 8)
-
-    def gy_copy(o):
-        return remote(g2.at[gmine], gy.at[o - 1], gy_send.at[o - 1], gy_recv.at[o - 1], col=lax.rem(c + o, YS))
-
-    def gz_back(o):
-        return remote(gf.at[gmine], gf.at[gmine], gz_send.at[1, o - 1], gz_recv.at[1, o - 1],
-                      row=row_of(x, lax.rem(z + o, ZS), k))
-
-    def g_back(o):
-        gp = lax.rem(g + o, GROUP)
-        ref = gf.at[ds(g * 64, 64)]
-        return remote(ref, ref, gg_send.at[1, o - 1], gg_recv.at[1, o - 1], row=row_of(gp // KS, z, gp % KS))
-
-    def gram_local():
-        own = [jnp.concatenate([yfull[p, ds(base(d, c), CH), :] for p in range(2)], axis=1) for d in range(2)]
-        own = jnp.concatenate(own, axis=0)
-        gram = dot3(split(own.T), split(own))
-        g2[0:256, :] = gram[:, :128]
-        g2[256:512, :] = gram[:, 128:]
-        start(g_copy, GROUP)
-
-    def g_stage1():
-        arrive(g_copy, GROUP)
-        rows = ds(g * 64, 64)
-        total = g2[rows, :]
+        return gp, row_of(gp // KS, z, gp % KS)
+
+    def g_copy(p):
+        def make(o):
+            gp, row = g_peer(o)
+            return remote(g2.at[p, g_rows(p, gp)], gg.at[p, o - 1, g_rows(p, 0)],
+                          gg_send.at[p, 0, o - 1], gg_recv.at[p, 0, o - 1], row=row)
+        return make
+
+    def gz_copy(p):
+        def make(o):
+            return remote(gz.at[p, z, g_rows(p, 0)], gz.at[p, z, g_rows(p, 0)], gz_send.at[p, o - 1], gz_recv.at[p, o - 1],
+                          row=row_of(x, lax.rem(z + o, ZS), k))
+        return make
+
+    def gz_from(p):
+        def make(o):
+            slot = gz.at[p, lax.rem(z + (ZS - o), ZS), g_rows(p, 0)]
+            return remote(slot, slot, gz_send.at[p, o - 1], gz_recv.at[p, o - 1], row=row_of(x, lax.rem(z + o, ZS), k))
+        return make
+
+    def gy_copy(p):
+        def make(o):
+            return remote(gt.at[p, g_rows(p, 0)], gy.at[p, o - 1, g_rows(p, 0)],
+                          gy_send.at[p, o - 1], gy_recv.at[p, o - 1], col=chunk(o))
+        return make
+
+    def g_back(p):
+        def make(o):
+            ref = gf.at[p, g_rows(p, g)]
+            return remote(ref, ref, gg_send.at[p, 1, o - 1], gg_recv.at[p, 1, o - 1], row=g_peer(o)[1])
+        return make
+
+    def own_rows(p):
+        return jnp.concatenate([yfull[p, ds(base(h, c), CH), :] for h in range(2)], axis=0)
+
+    def gram_local(p):
+        own = own_rows(p)
+        right = split(own) if p == 0 else split(jnp.concatenate([own_rows(0), own], axis=1))
+        gram = dot3(split(own.T), right)
+        for q in range(p + 1):
+            g2[p, q * 128:(q + 1) * 128, :] = gram[:, q * 128:(q + 1) * 128]
+        start(g_copy(p), GROUP)
+
+    def g_stage1(p):
+        arrive(g_copy(p), GROUP)
+        total = g2[p, g_rows(p, g), :]
         for o in range(GROUP - 1):
-            total = total + gg[o]
-        g2[rows, :] = total
-        start(gz_copy, ZS)
-
-    def g_stage2():
-        arrive(gz_copy, ZS)
-        total = g2[gmine, :]
-        for o in range(ZS - 1):
-            total = total + gz[o]
-        g2[gmine, :] = total
-        start(gy_copy, YS)
-
-    def g_stage3():
-        arrive(gy_copy, YS)
-        gf[gmine, :] = (g2[gmine, :] + gy[1]) + (gy[0] + gy[2])
-        start(gz_back, ZS)
-
-    def g_stage4():
-        arrive(gz_back, ZS)
-        start(g_back, GROUP)
-
-    def g_stage5():
-        arrive(g_back, GROUP)
-
-    def product(p, d, j, first):
-        rows = ds(base(d, j), CH)
+            total = total + gg[p, o, g_rows(p, 0), :]
+        gz[p, z, g_rows(p, 0), :] = total
+        start(gz_copy(p), ZS)
+
+    def g_stage2(p):
+        arrive(gz_from(p), ZS)
+        total = gz[p, 0, g_rows(p, 0), :]
+        for o in range(1, ZS):
+            total = total + gz[p, o, g_rows(p, 0), :]
+        gt[p, g_rows(p, 0), :] = total
+        start(gy_copy(p), YS)
+
+    def g_stage3(p):
+        arrive(gy_copy(p), YS)
+        rows = g_rows(p, 0)
+        gf[p, g_rows(p, g), :] = (gt[p, rows, :] + gy[p, 1, rows, :]) + (gy[p, 0, rows, :] + gy[p, 2, rows, :])
+        start(g_back(p), GROUP)
+
+    def g_stage4(p):
+        arrive(g_back(p), GROUP)
+
+    def product(p, h, step, first=False):
+        rows = ds(base(h, chunk(step)), CH)
         left = split(yfull[p, rows, :].T)
         for t in range(4):
             lanes = slice(t * 256, (t + 1) * 256)
             part = dot3(left, (ahi[rows, lanes], alo[rows, lanes]))
-            for h in range(2):
-                out = slice((2 * t + h) * 128, (2 * t + h + 1) * 128)
+            for q in range(2):
+                out = slice((2 * t + q) * 128, (2 * t + q + 1) * 128)
                 if first:
-                    c2[p, out, :] = part[:, h * 128:(h + 1) * 128]
+                    c2[p, out, :] = part[:, q * 128:(q + 1) * 128]
                 else:
-                    c2[p, out, :] += part[:, h * 128:(h + 1) * 128]
-
-    def step_products(p, s):
-        for d in range(2):
-            product(p, d, lax.rem(c + (YS - 1 - s if d == 0 else 1 + s), YS), False)
+                    c2[p, out, :] += part[:, q * 128:(q + 1) * 128]
 
     half = k * 512
     mine = ds(half, 512)
@@ -325,12 +360,12 @@
         return same.astype(F32)
 
     def factor_start0():
-        work[0, :, :128] = gf[0:128, :] * INV_TOTAL
+        work[0, :, :128] = gf[0, 0:128, :] * INV_TOTAL
         work[0, :, 128:] = eye()
 
     def factor_start1():
-        cross = fdot(work[0, :, 128:], gf[256:384, :] * INV_TOTAL)
-        work[1, :, :128] = gf[384:512, :] * INV_TOTAL - fdot(cross.T, cross)
+        cross = fdot(work[0, :, 128:], gf[1, 0:128, :].T * INV_TOTAL)
+        work[1, :, :128] = gf[1, 128:256, :] * INV_TOTAL - fdot(cross.T, cross)
         work[1, :, 128:] = eye()
         inv[:128, 128:] = cross
 
@@ -357,97 +392,102 @@
             copy.start()
             basis_copies.append(copy)
 
-    def ag_pass(p, s, h):
+    def gathered_first(p):
         for d in range(2):
-            ag_copy(p, d, s, h).wait_recv()
-            if s < YS - 2:
-                go(ag_copy(p, d, s + 1, h))
-
+            gather(p, d, d).wait_recv()
+            go(gather_on(p, d))
+
+    def gathered_second(p):
+        for d in range(2):
+            gather(p, d, 1 - d).wait_recv()
+
+    def gathered_last(p):
+        for d in range(2):
+            gather_on(p, d).wait_recv()
+
+    for unit in units[:4]:
+        sketch(*unit)
+    pl.semaphore_wait(barrier, (YS - 1) + (GROUP - 1) + (ZS - 1))
+    for make, p in ((relay, 0), (relay, 1), (direct, 0)):
+        for d in range(2):
+            go(make(p, d))
+    for unit in units[4:]:
+        sketch(*unit)
+    pass_on(0)
+    pass_on(1)
     for d in range(2):
-        sketch(d, 0)
-        if d == 0:
-            pl.semaphore_wait(barrier, (YS - 1) + (GROUP - 1) + (ZS - 1))
-        for p in range(2):
-            go(rs_copy(p, d, 0))
+        go(direct(1, d))
+    own_sum(0)
     for d in range(2):
-        sketch(d, 1)
-    for s in range(1, YS):
-        for p in range(2):
-            for d in range(2):
-                rs_copy(p, d, s - 1).wait_recv()
-                rows = ds(base(d, chunk(d, s)), CH)
-                if s < YS - 1:
-                    rs[p, d, s - 1] = rs[p, d, s - 1] + ypart[p, rows, :]
-                    go(rs_copy(p, d, s))
-                else:
-                    yfull[p, rows, :] = rs[p, d, s - 1] + ypart[p, rows, :]
-                    if p == 0:
-                        for h in range(2):
-                            go(ag_copy(0, d, 0, h))
-        if s < YS - 1:
-            for d in range(2):
-                sketch(d, s + 1)
-
-    gram_local()
-    product(0, 0, c, True)
-    product(0, 1, c, False)
-    ag_pass(0, 0, 0)
-    g_stage1()
-    ag_pass(0, 0, 1)
-    g_stage2()
-    step_products(0, 0)
-    ag_pass(0, 1, 0)
-    g_stage3()
-    ag_pass(0, 1, 1)
-    for h in range(2):
-        for d in range(2):
-            go(ag_copy(1, d, 0, h))
-    step_products(0, 1)
-    g_stage4()
-    ag_pass(0, 2, 0)
-    ag_pass(0, 2, 1)
-    step_products(0, 2)
+        go(gather(0, d, d))
+    for d in range(2):
+        go(gather(0, d, 1 - d))
+    gram_local(0)
+    product(0, 0, 0, True)
+    product(0, 1, 0)
+    g_stage1(0)
+    own_sum(1)
+    for d in range(2):
+        go(gather(1, d, d))
+    gram_local(1)
+    product(1, 0, 0, True)
+    product(1, 1, 0)
+    gathered_first(0)
+    for d in range(2):
+        go(gather(1, d, 1 - d))
+    product(0, 0, 3)
+    product(0, 1, 1)
+    g_stage1(1)
+    g_stage2(0)
+    gathered_second(0)
+    product(0, 1, 3)
+    product(0, 0, 1)
+    gathered_last(0)
+    product(0, 0, 2)
+    product(0, 1, 2)
     go(core_copy(0))
-    g_stage5()
+    gathered_first(1)
+    c_stage1(0)
+    g_stage3(0)
+    product(1, 0, 3)
+    product(1, 1, 1)
+    g_stage2(1)
+    gathered_second(1)
+    product(1, 1, 3)
+    product(1, 0, 1)
+    c_stage2(0)
+    gathered_last(1)
+    product(1, 0, 2)
+    product(1, 1, 2)
+    go(core_copy(1))
+    g_stage4(0)
     factor_start0()
+    c_stage1(1)
+    g_stage3(1)
     eliminate(work.at[0], 0)
-    c_stage1(0)
-    ag_pass(1, 0, 0)
-    product(1, 0, c, True)
-    product(1, 1, c, False)
-    ag_pass(1, 0, 1)
     eliminate(work.at[0], 4)
+    c_stage3(0)
     eliminate(work.at[0], 8)
-    step_products(1, 0)
-    ag_pass(1, 1, 0)
-    c_stage2(0)
+    c_stage2(1)
     eliminate(work.at[0], 12)
-    ag_pass(1, 1, 1)
+    g_stage4(1)
     factor_start1()
+    c_stage4(0)
     eliminate(work.at[1], 0)
-    c_stage3(0)
-    step_products(1, 1)
-    ag_pass(1, 2, 0)
-    ag_pass(1, 2, 1)
-    step_products(1, 2)
-    go(core_copy(1))
-    c_stage4(0)
+    c_stage3(1)
     eliminate(work.at[1], 4)
-    c_stage1(1)
     eliminate(work.at[1], 8)
     eliminate(work.at[1], 12)
     c_stage5(0)
-    c_stage2(1)
     factor_end()
+    c_stage4(1)
     c_stage6(0)
     first = dot3(split(inv[:, :128]), split(gathered(0)))
     obuf[:128, :] = first[:128, :] * INV_ROOT
     obuf[128:, :] = first[128:, :]
     coeff_copy0 = pltpu.make_async_copy(obuf.at[0:128], coeff_out.at[0:128], out_sem.at[8])
     coeff_copy0.start()
-    c_stage3(1)
     bases()
-    c_stage4(1)
     c_stage5(1)
     c_stage6(1)
     last = dot3(split(inv[128:, 128:]), split(gathered(1)))
@@ -476,12 +516,13 @@
             vmem((2, 2, 3, CH, 128), F32), vmem((2, ROWS, 128), F32),
             vmem((2, 1024, 128), F32), vmem((2, 1024, 128), F32), vmem((2, 512, 128), F32),
             vmem((2, 3, 128, 128), F32), vmem((2, 7, 16, 128), F32),
-            vmem((512, 128), F32), vmem((512, 128), F32), vmem((7, 64, 128), F32),
-            vmem((7, 8, 128), F32), vmem((3, 8, 128), F32), vmem((2, 128, 256), F32), vmem((256, 256), F32),
+            vmem((2, 256, 128), F32), vmem((2, 256, 128), F32), vmem((2, 7, 32, 128), F32),
+            vmem((2, ZS, 32, 128), F32), vmem((2, 3, 32, 128), F32), vmem((2, 32, 128), F32),
+            vmem((2, 128, 256), F32), vmem((256, 256), F32),
             vmem((ROWS, 256), F32), vmem((256, COLS), F32),
-            dma((10,)), dma((2, 2, 3)), dma((2, 2, 3)), dma((2, 2, 3, 2)), dma((2, 2, 3, 2)),
+            dma((10,)), dma((2, 2, 3)), dma((2, 2, 3)), dma((2, 2, 3)), dma((2, 2, 3)),
             dma((2, 2)), dma((2, 2)), dma((2, 2, 3)), dma((2, 2, 3)), dma((2, 2, 7)), dma((2, 2, 7)),
-            dma((2, 7)), dma((2, 7)), dma((2, 7)), dma((2, 7)), dma((3,)), dma((3,)), dma((10,))],
+            dma((2, 2, 7)), dma((2, 2, 7)), dma((2, 7)), dma((2, 7)), dma((2, 3)), dma((2, 3)), dma((10,))],
         compiler_params=pltpu.CompilerParams(collective_id=0, has_side_effects=True, vmem_limit_bytes=56 << 20),
     )(snapshots, tests)
 

time: 104 us -> 86 us (0.83)
  Pallas kernels: 99.5 us -> 81.1 us
    pallas_call x1, Pallas kernels: 99.5 us -> 81.1 us  [per_device(): pl.pallas_call(comm_kernel, out_shape=(jax.ShapeDtypeStruct((ROWS, 256),...]
where the time goes in v2:
time: 86 us; the launch traced here: 85.9 us
  Pallas kernels  81.1 us (94%)
  local copies, waits for them, and re-layouts  4.11 us (5%)
    pallas_call x1, Pallas kernels, per_device(): pl.pallas_call(comm_kernel, out_shape=(jax.ShapeDtypeStruct((ROWS, 256),...  81.1 us
    unnamed x4, local copies, waits for them, and re-layouts  4.11 us

profile of v2, /device:TPU:1, one launch (start us, length us, event | category | flops | bytes accessed | tf_op | source)
XLA Modules:
  0.0 85.9 jit_solution(13475532708602210249)
XLA Ops:
  0.6 81.1 %shard_map.41 = (f32[2048,256]{1,0:T(8,128)}, f32[256,1024]{1,0:T(8,128)}) custom-call(f32[2048,1024]{1,0:T(8,128)} %a_hbm.1, f32[2,1024,128]{2,1,0:T(8,128)} %t_hbm.1), custom_call_target="tpu_custom_call" | custom-call | tf_op jit(solution)/shard_map/pallas_call | solution.py:508
  81.8 0.0 copy-start
  81.8 3.1 %copy.6 = f32[2048,256]{1,0:T(8,128)} copy(f32[2048,256]{1,0:T(8,128)} %get-tuple-element.4) | data formatting | bytes 4194304
  84.9 0.0 copy-done
  84.9 1.0 %copy.7 = f32[256,1024]{1,0:T(8,128)} copy(f32[256,1024]{1,0:T(8,128)S(1)} %copy-done) | data formatting | bytes 2097152
Async XLA Ops:
  81.8 3.1 %copy-start = (f32[256,1024]{1,0:T(8,128)S(1)}, f32[256,1024]{1,0:T(8,128)}, u32[]{:S(2)}) copy-start(f32[256,1024]{1,0:T(8,128)} %get-tuple-element.5) | copy-start | bytes 3145732

commit v3 on v2

--- a/solution.py
+++ b/solution.py
@@ -1,3 +1,4 @@
+import functools
 import math
 
 import jax
@@ -14,7 +15,6 @@
 ROWS = 2048
 COLS = 1024
 CH = 256
-GROUP = XS * KS
 TOTAL = float(ROWS * XS * ZS * KS)
 INV_TOTAL = 1.0 / TOTAL
 INV_ROOT = 1.0 / math.sqrt(TOTAL)
@@ -85,17 +85,16 @@
 
 
 def comm_kernel(
-    a_hbm, t_hbm, basis_out, coeff_out,
+    a_hbm, t_hbm, bbuf, obuf,
     abuf, tbuf, ahi, alo, th, tl, ypart, rs, yfull,
-    c2, cf, ccore, cx, cz, g2, gf, gg, gz, gy, gt, work, inv, bbuf, obuf,
+    c2, cf, ccore, cx, cz, g2, gf, gk, gx, gz, gy, gt, work, inv,
     load_sem, rs_send, rs_recv, ag_send, ag_recv,
     core_send, core_recv, x_send, x_recv, z_send, z_recv,
-    gg_send, gg_recv, gz_send, gz_recv, gy_send, gy_recv, out_sem,
+    inv_sem, gk_send, gk_recv, gx_send, gx_recv, gz_send, gz_recv, gy_send, gy_recv,
 ):
     r = lax.axis_index("row")
     c = lax.axis_index("col")
     x, z, k = r // (ZS * KS), (r // KS) % ZS, r % KS
-    g = x * KS + k
 
     def row_of(xx, zz, kk):
         return xx * (ZS * KS) + zz * KS + kk
@@ -112,25 +111,33 @@
             device_id=where, device_id_type=MESH)
 
     sends = []
+    role_sends = ([], [])
 
     def go(copy):
         copy.start()
         sends.append(copy)
 
-    def start(make, count):
-        for o in range(1, count):
-            go(make(o))
+    def go_role(make, core):
+        make().start()
+        role_sends[core].append(make)
+
+    def start(make, count, core):
+        for o in sorted(range(1, count), key=lambda o: -min(o, count - o)):
+            go_role(functools.partial(make, o), core)
 
     def arrive(make, count):
         for o in range(1, count):
             make(o).wait_recv()
 
+    def role(core):
+        return pl.when(k == core)
+
     barrier = pltpu.get_barrier_semaphore()
-    for o in range(1, ZS):
+    for o in (4, 3, 5, 2, 6, 1, 7):
         pl.semaphore_signal(barrier, inc=1, device_id={"row": row_of(x, lax.rem(z + o, ZS), k)}, device_id_type=MESH)
-    for o in range(1, GROUP):
-        gp = lax.rem(g + o, GROUP)
-        pl.semaphore_signal(barrier, inc=1, device_id={"row": row_of(gp // KS, z, gp % KS)}, device_id_type=MESH)
+    for o in range(1, XS):
+        pl.semaphore_signal(barrier, inc=1, device_id={"row": row_of(lax.rem(x + o, XS), z, k)}, device_id_type=MESH)
+    pl.semaphore_signal(barrier, inc=1, device_id={"row": row_of(x, z, 1 - k)}, device_id_type=MESH)
     for o in range(1, YS):
         pl.semaphore_signal(barrier, inc=1, device_id={"col": chunk(o)}, device_id_type=MESH)
 
@@ -197,24 +204,32 @@
         ypart[0, rows, :] = part[:, :128]
         ypart[1, rows, :] = part[:, 128:]
 
-    def g_rows(p, index):
-        return ds(index * (16 * (p + 1)), 16 * (p + 1))
-
-    def g_peer(o):
-        gp = lax.rem(g + o, GROUP)
-        return gp, row_of(gp // KS, z, gp % KS)
-
-    def g_copy(p):
-        def make(o):
-            gp, row = g_peer(o)
-            return remote(g2.at[p, g_rows(p, gp)], gg.at[p, o - 1, g_rows(p, 0)],
-                          gg_send.at[p, 0, o - 1], gg_recv.at[p, 0, o - 1], row=row)
+    def g_rows(p, index, size=32):
+        return ds(index * (size * (p + 1)), size * (p + 1))
+
+    core_peer = row_of(x, z, 1 - k)
+
+    def gk_copy(p):
+        return remote(g2.at[p, g_rows(p, 0, 128)], gk.at[p, g_rows(p, 0, 128)], gk_send.at[p], gk_recv.at[p], row=core_peer)
+
+    def gx_copy(p):
+        def make(o):
+            xp = lax.rem(x + o, XS)
+            return remote(g2.at[p, g_rows(p, xp)], gx.at[p, o - 1, g_rows(p, 0)],
+                          gx_send.at[p, 0, o - 1], gx_recv.at[p, 0, o - 1], row=row_of(xp, z, k))
+        return make
+
+    def gx_back(p):
+        def make(o):
+            ref = gf.at[p, g_rows(p, x)]
+            return remote(ref, ref, gx_send.at[p, 1, o - 1], gx_recv.at[p, 1, o - 1],
+                          row=row_of(lax.rem(x + o, XS), z, k))
         return make
 
     def gz_copy(p):
         def make(o):
-            return remote(gz.at[p, z, g_rows(p, 0)], gz.at[p, z, g_rows(p, 0)], gz_send.at[p, o - 1], gz_recv.at[p, o - 1],
-                          row=row_of(x, lax.rem(z + o, ZS), k))
+            slot = gz.at[p, z, g_rows(p, 0)]
+            return remote(slot, slot, gz_send.at[p, o - 1], gz_recv.at[p, o - 1], row=row_of(x, lax.rem(z + o, ZS), k))
         return make
 
     def gz_from(p):
@@ -227,12 +242,6 @@
         def make(o):
             return remote(gt.at[p, g_rows(p, 0)], gy.at[p, o - 1, g_rows(p, 0)],
                           gy_send.at[p, o - 1], gy_recv.at[p, o - 1], col=chunk(o))
-        return make
-
-    def g_back(p):
-        def make(o):
-            ref = gf.at[p, g_rows(p, g)]
-            return remote(ref, ref, gg_send.at[p, 1, o - 1], gg_recv.at[p, 1, o - 1], row=g_peer(o)[1])
         return make
 
     def own_rows(p):
@@ -244,32 +253,50 @@
         gram = dot3(split(own.T), right)
         for q in range(p + 1):
             g2[p, q * 128:(q + 1) * 128, :] = gram[:, q * 128:(q + 1) * 128]
-        start(g_copy(p), GROUP)
-
-    def g_stage1(p):
-        arrive(g_copy(p), GROUP)
-        total = g2[p, g_rows(p, g), :]
-        for o in range(GROUP - 1):
-            total = total + gg[p, o, g_rows(p, 0), :]
-        gz[p, z, g_rows(p, 0), :] = total
-        start(gz_copy(p), ZS)
-
-    def g_stage2(p):
-        arrive(gz_from(p), ZS)
-        total = gz[p, 0, g_rows(p, 0), :]
-        for o in range(1, ZS):
-            total = total + gz[p, o, g_rows(p, 0), :]
-        gt[p, g_rows(p, 0), :] = total
-        start(gy_copy(p), YS)
-
-    def g_stage3(p):
-        arrive(gy_copy(p), YS)
-        rows = g_rows(p, 0)
-        gf[p, g_rows(p, g), :] = (gt[p, rows, :] + gy[p, 1, rows, :]) + (gy[p, 0, rows, :] + gy[p, 2, rows, :])
-        start(g_back(p), GROUP)
-
-    def g_stage4(p):
-        arrive(g_back(p), GROUP)
+
+        @role(0)
+        def _():
+            go_role(functools.partial(gk_copy, p), 0)
+
+    def g_core(p):
+        @role(1)
+        def _():
+            gk_copy(p).wait_recv()
+            rows = g_rows(p, 0, 128)
+            g2[p, rows, :] = g2[p, rows, :] + gk[p, rows, :]
+            start(gx_copy(p), XS, 1)
+
+    def g_x(p):
+        @role(1)
+        def _():
+            arrive(gx_copy(p), XS)
+            rows = g_rows(p, 0)
+            total = (g2[p, g_rows(p, x), :] + gx[p, 1, rows, :]) + (gx[p, 0, rows, :] + gx[p, 2, rows, :])
+            gz[p, z, rows, :] = total
+            start(gz_copy(p), ZS, 1)
+
+    def g_z(p):
+        @role(1)
+        def _():
+            arrive(gz_from(p), ZS)
+            total = gz[p, 0, g_rows(p, 0), :]
+            for o in range(1, ZS):
+                total = total + gz[p, o, g_rows(p, 0), :]
+            gt[p, g_rows(p, 0), :] = total
+            start(gy_copy(p), YS, 1)
+
+    def g_y(p):
+        @role(1)
+        def _():
+            arrive(gy_copy(p), YS)
+            rows = g_rows(p, 0)
+            gf[p, g_rows(p, x), :] = (gt[p, rows, :] + gy[p, 1, rows, :]) + (gy[p, 0, rows, :] + gy[p, 2, rows, :])
+            start(gx_back(p), XS, 1)
+
+    def g_x_back(p):
+        @role(1)
+        def _():
+            arrive(gx_back(p), XS)
 
     def product(p, h, step, first=False):
         rows = ds(base(h, chunk(step)), CH)
@@ -284,30 +311,26 @@
                 else:
                     c2[p, out, :] += part[:, q * 128:(q + 1) * 128]
 
-    half = k * 512
-    mine = ds(half, 512)
-    quarter = half + x * 128
-    piece = ds(quarter + z * 16, 16)
-    core_peer = row_of(x, z, 1 - k)
+    quarter = x * 256
+    piece = ds(quarter + z * 32, 32)
 
     def core_copy(p):
-        return remote(c2.at[p, ds((1 - k) * 512, 512)], ccore.at[p], core_send.at[p, 0], core_recv.at[p, 0],
-                      row=core_peer)
+        return remote(c2.at[p], ccore.at[p], core_send.at[p, 0], core_recv.at[p, 0], row=core_peer)
 
     def core_back(p):
-        return remote(cf.at[p, mine], cf.at[p, mine], core_send.at[p, 1], core_recv.at[p, 1], row=core_peer)
+        return remote(cf.at[p], cf.at[p], core_send.at[p, 1], core_recv.at[p, 1], row=core_peer)
 
     def x_copy(p):
         def make(o):
             xp = lax.rem(x + o, XS)
-            return remote(c2.at[p, ds(half + xp * 128, 128)], cx.at[p, o - 1],
+            return remote(c2.at[p, ds(xp * 256, 256)], cx.at[p, o - 1],
                           x_send.at[p, 0, o - 1], x_recv.at[p, 0, o - 1], row=row_of(xp, z, k))
         return make
 
     def z_copy(p):
         def make(o):
             zp = lax.rem(z + o, ZS)
-            return remote(c2.at[p, ds(quarter + zp * 16, 16)], cz.at[p, o - 1],
+            return remote(c2.at[p, ds(quarter + zp * 32, 32)], cz.at[p, o - 1],
                           z_send.at[p, 0, o - 1], z_recv.at[p, 0, o - 1], row=row_of(x, zp, k))
         return make
 
@@ -319,40 +342,57 @@
 
     def x_back(p):
         def make(o):
-            ref = cf.at[p, ds(quarter, 128)]
+            ref = cf.at[p, ds(quarter, 256)]
             return remote(ref, ref, x_send.at[p, 1, o - 1], x_recv.at[p, 1, o - 1],
                           row=row_of(lax.rem(x + o, XS), z, k))
         return make
 
-    def c_stage1(p):
-        core_copy(p).wait_recv()
-        c2[p, mine, :] += ccore[p]
-        start(x_copy(p), XS)
-
-    def c_stage2(p):
-        arrive(x_copy(p), XS)
-        rows = ds(quarter, 128)
-        c2[p, rows, :] = (c2[p, rows, :] + cx[p, 0]) + (cx[p, 1] + cx[p, 2])
-        start(z_copy(p), ZS)
-
-    def c_stage3(p):
-        arrive(z_copy(p), ZS)
-        total = c2[p, piece, :]
-        for o in range(ZS - 1):
-            total = total + cz[p, o]
-        cf[p, piece, :] = total
-        start(z_back(p), ZS)
-
-    def c_stage4(p):
-        arrive(z_back(p), ZS)
-        start(x_back(p), XS)
-
-    def c_stage5(p):
-        arrive(x_back(p), XS)
-        go(core_back(p))
-
-    def c_stage6(p):
-        core_back(p).wait_recv()
+    def c_send(p):
+        @role(1)
+        def _():
+            go_role(functools.partial(core_copy, p), 1)
+
+    def c_core(p):
+        @role(0)
+        def _():
+            core_copy(p).wait_recv()
+            c2[p] = c2[p] + ccore[p]
+            start(x_copy(p), XS, 0)
+
+    def c_x(p):
+        @role(0)
+        def _():
+            arrive(x_copy(p), XS)
+            rows = ds(quarter, 256)
+            c2[p, rows, :] = (c2[p, rows, :] + cx[p, 0]) + (cx[p, 1] + cx[p, 2])
+            start(z_copy(p), ZS, 0)
+
+    def c_z(p):
+        @role(0)
+        def _():
+            arrive(z_copy(p), ZS)
+            total = c2[p, piece, :]
+            for o in range(ZS - 1):
+                total = total + cz[p, o]
+            cf[p, piece, :] = total
+            start(z_back(p), ZS, 0)
+
+    def c_z_back(p):
+        @role(0)
+        def _():
+            arrive(z_back(p), ZS)
+            start(x_back(p), XS, 0)
+
+    def c_x_back(p):
+        @role(0)
+        def _():
+            arrive(x_back(p), XS)
+            go_role(functools.partial(core_back, p), 0)
+
+    def c_core_back(p):
+        @role(1)
+        def _():
+            core_back(p).wait_recv()
 
     def eye():
         shape = (128, 128)
@@ -377,10 +417,11 @@
         inv[128:, :128] = corner
         inv[128:, 128:] = inv1
 
+    def inverse_copy():
+        return remote(inv, inv, inv_sem.at[0], inv_sem.at[1], row=core_peer)
+
     def gathered(p):
         return jnp.concatenate([cf[p, t * 128:(t + 1) * 128, :] for t in range(8)], axis=1)
-
-    basis_copies = []
 
     def bases():
         across = split(inv[...].T)
@@ -388,9 +429,6 @@
             rows = slice(i * CH, (i + 1) * CH)
             y = jnp.concatenate([yfull[0, rows, :], yfull[1, rows, :]], axis=1)
             bbuf[rows, :] = dot3(split(y), across)
-            copy = pltpu.make_async_copy(bbuf.at[rows], basis_out.at[rows], out_sem.at[i])
-            copy.start()
-            basis_copies.append(copy)
 
     def gathered_first(p):
         for d in range(2):
@@ -407,16 +445,20 @@
 
     for unit in units[:4]:
         sketch(*unit)
-    pl.semaphore_wait(barrier, (YS - 1) + (GROUP - 1) + (ZS - 1))
-    for make, p in ((relay, 0), (relay, 1), (direct, 0)):
+    pl.semaphore_wait(barrier, (YS - 1) + (XS - 1) + (KS - 1) + (ZS - 1))
+    for make in (relay, direct):
         for d in range(2):
-            go(make(p, d))
-    for unit in units[4:]:
+            go(make(0, d))
+    for unit in units[4:6]:
+        sketch(*unit)
+    for d in range(2):
+        go(relay(1, d))
+    for unit in units[6:]:
         sketch(*unit)
     pass_on(0)
-    pass_on(1)
     for d in range(2):
         go(direct(1, d))
+    pass_on(1)
     own_sum(0)
     for d in range(2):
         go(gather(0, d, d))
@@ -425,11 +467,13 @@
     gram_local(0)
     product(0, 0, 0, True)
     product(0, 1, 0)
-    g_stage1(0)
+    g_core(0)
     own_sum(1)
     for d in range(2):
         go(gather(1, d, d))
     gram_local(1)
+    g_x(0)
+    g_core(1)
     product(1, 0, 0, True)
     product(1, 1, 0)
     gathered_first(0)
@@ -437,69 +481,85 @@
         go(gather(1, d, 1 - d))
     product(0, 0, 3)
     product(0, 1, 1)
-    g_stage1(1)
-    g_stage2(0)
     gathered_second(0)
     product(0, 1, 3)
     product(0, 0, 1)
+    g_x(1)
+    g_z(0)
     gathered_last(0)
     product(0, 0, 2)
     product(0, 1, 2)
-    go(core_copy(0))
+    c_send(0)
+    c_core(0)
     gathered_first(1)
-    c_stage1(0)
-    g_stage3(0)
+    g_y(0)
     product(1, 0, 3)
     product(1, 1, 1)
-    g_stage2(1)
+    g_z(1)
     gathered_second(1)
     product(1, 1, 3)
     product(1, 0, 1)
-    c_stage2(0)
+    g_x_back(0)
+    c_x(0)
+    g_y(1)
+
+    @role(1)
+    def _():
+        factor_start0()
+        eliminate(work.at[0], 0)
+
     gathered_last(1)
     product(1, 0, 2)
     product(1, 1, 2)
-    go(core_copy(1))
-    g_stage4(0)
-    factor_start0()
-    c_stage1(1)
-    g_stage3(1)
-    eliminate(work.at[0], 0)
-    eliminate(work.at[0], 4)
-    c_stage3(0)
-    eliminate(work.at[0], 8)
-    c_stage2(1)
-    eliminate(work.at[0], 12)
-    g_stage4(1)
-    factor_start1()
-    c_stage4(0)
-    eliminate(work.at[1], 0)
-    c_stage3(1)
-    eliminate(work.at[1], 4)
-    eliminate(work.at[1], 8)
-    eliminate(work.at[1], 12)
-    c_stage5(0)
-    factor_end()
-    c_stage4(1)
-    c_stage6(0)
-    first = dot3(split(inv[:, :128]), split(gathered(0)))
-    obuf[:128, :] = first[:128, :] * INV_ROOT
-    obuf[128:, :] = first[128:, :]
-    coeff_copy0 = pltpu.make_async_copy(obuf.at[0:128], coeff_out.at[0:128], out_sem.at[8])
-    coeff_copy0.start()
+    c_send(1)
+
+    def first():
+        both = dot3(split(inv[:, :128]), split(gathered(0)))
+        obuf[:128, :] = both[:128, :] * INV_ROOT
+        obuf[128:, :] = both[128:, :]
+
+    c_core(1)
+    c_z(0)
+    c_x(1)
+    c_z_back(0)
+    c_z(1)
+    c_x_back(0)
+    c_z_back(1)
+
+    @role(1)
+    def _():
+        for i in (4, 8, 12):
+            eliminate(work.at[0], i)
+
+    g_x_back(1)
+
+    @role(1)
+    def _():
+        factor_start1()
+        for i in (0, 4, 8, 12):
+            eliminate(work.at[1], i)
+        factor_end()
+        go_role(inverse_copy, 1)
+
+    @role(0)
+    def _():
+        inverse_copy().wait_recv()
+
+    c_core_back(0)
     bases()
-    c_stage5(1)
-    c_stage6(1)
+    first()
+    c_x_back(1)
+    c_core_back(1)
     last = dot3(split(inv[128:, 128:]), split(gathered(1)))
     obuf[128:, :] = (obuf[128:, :] + last) * INV_ROOT
-    coeff_copy1 = pltpu.make_async_copy(obuf.at[128:256], coeff_out.at[128:256], out_sem.at[9])
-    coeff_copy1.start()
+    for core in range(2):
+        @role(core)
+        def _():
+            for make in role_sends[core]:
+                make().wait_send()
+
     for copy in sends:
         copy.wait_send()
-    for copy in basis_copies:
-        copy.wait()
-    coeff_copy0.wait()
-    coeff_copy1.wait()
 
 
 def per_device(snapshots, tests):
@@ -507,23 +567,22 @@
     any_spec = pl.BlockSpec(memory_space=pl.ANY)
     return pl.pallas_call(
         comm_kernel,
-        out_shape=(jax.ShapeDtypeStruct((ROWS, 256), F32), jax.ShapeDtypeStruct((256, COLS), F32)),
+        out_shape=(vmem((ROWS, 256), F32), vmem((256, COLS), F32)),
         in_specs=[any_spec, any_spec],
-        out_specs=(any_spec, any_spec),
+        out_specs=(pl.BlockSpec(memory_space=vmem), pl.BlockSpec(memory_space=vmem)),
         scratch_shapes=[
             vmem((ROWS, COLS), F32), vmem((2, COLS, 128), F32), vmem((ROWS, COLS), BF16), vmem((ROWS, COLS), BF16),
             vmem((COLS, 256), BF16), vmem((COLS, 256), BF16), vmem((2, ROWS, 128), F32),
             vmem((2, 2, 3, CH, 128), F32), vmem((2, ROWS, 128), F32),
-            vmem((2, 1024, 128), F32), vmem((2, 1024, 128), F32), vmem((2, 512, 128), F32),
-            vmem((2, 3, 128, 128), F32), vmem((2, 7, 16, 128), F32),
-            vmem((2, 256, 128), F32), vmem((2, 256, 128), F32), vmem((2, 7, 32, 128), F32),
-            vmem((2, ZS, 32, 128), F32), vmem((2, 3, 32, 128), F32), vmem((2, 32, 128), F32),
+            vmem((2, 1024, 128), F32), vmem((2, 1024, 128), F32), vmem((2, 1024, 128), F32),
+            vmem((2, 3, 256, 128), F32), vmem((2, 7, 32, 128), F32),
+            vmem((2, 256, 128), F32), vmem((2, 256, 128), F32), vmem((2, 256, 128), F32), vmem((2, 3, 64, 128), F32),
+            vmem((2, ZS, 64, 128), F32), vmem((2, 3, 64, 128), F32), vmem((2, 64, 128), F32),
             vmem((2, 128, 256), F32), vmem((256, 256), F32),
-            vmem((ROWS, 256), F32), vmem((256, COLS), F32),
             dma((10,)), dma((2, 2, 3)), dma((2, 2, 3)), dma((2, 2, 3)), dma((2, 2, 3)),
-            dma((2, 2)), dma((2, 2)), dma((2, 2, 3)), dma((2, 2, 3)), dma((2, 2, 7)), dma((2, 2, 7)),
-            dma((2, 2, 7)), dma((2, 2, 7)), dma((2, 7)), dma((2, 7)), dma((2, 3)), dma((2, 3)), dma((10,))],
-        compiler_params=pltpu.CompilerParams(collective_id=0, has_side_effects=True, vmem_limit_bytes=56 << 20),
+            dma((2, 2)), dma((2, 2)), dma((2, 2, 3)), dma((2, 2, 3)), dma((2, 2, 7)), dma((2, 2, 7)), dma((2,)),
+            dma((2,)), dma((2,)), dma((2, 2, 3)), dma((2, 2, 3)), dma((2, 7)), dma((2, 7)), dma((2, 3)), dma((2, 3))],
+        compiler_params=pltpu.CompilerParams(collective_id=0, has_side_effects=True, vmem_limit_bytes=52 << 20),
     )(snapshots, tests)
 
 

time: 86 us -> 81.4 us (0.947)
  Pallas kernels: 81.1 us -> 78.4 us
  local copies, waits for them, and re-layouts: 4.11 us -> 2.29 us
    pallas_call x1, Pallas kernels: 81.1 us -> 78.4 us  [per_device(): pl.pallas_call(comm_kernel, out_shape=(vmem((ROWS, 256), F32), vmem((256,...]
    unnamed x4 -> x2, local copies, waits for them, and re-layouts: 4.11 us -> 2.29 us
where the time goes in v3:
time: 81.4 us
  Pallas kernels  78.4 us (96%)
  local copies, waits for them, and re-layouts  2.29 us (3%)
    pallas_call x1, Pallas kernels, per_device(): pl.pallas_call(comm_kernel, out_shape=(vmem((ROWS, 256), F32), vmem((256,...  78.4 us
    unnamed x2, local copies, waits for them, and re-layouts  2.29 us

profile of v3, /device:TPU:1, one launch (start us, length us, event | category | flops | bytes accessed | tf_op | source)
XLA Modules:
  0.0 81.4 jit_solution(5500071098795303470)
XLA Ops:
  0.6 78.4 %shard_map.41 = (f32[2048,256]{1,0:T(8,128)S(1)}, f32[256,1024]{1,0:T(8,128)S(1)}) custom-call(f32[2048,1024]{1,0:T(8,128)} %a_hbm.1, f32[2,1024,128]{2,1,0:T(8,128)} %t_hbm.1), custom_call_target="tpu_custom_call" | custom-call | tf_op jit(solution)/shard_map/pallas_call | solution.py:568
  79.1 1.3 %copy.6 = f32[2048,256]{1,0:T(8,128)} copy(f32[2048,256]{1,0:T(8,128)S(1)} %get-tuple-element.2) | data formatting | bytes 4194304
  80.4 1.0 %copy.7 = f32[256,1024]{1,0:T(8,128)} copy(f32[256,1024]{1,0:T(8,128)S(1)} %get-tuple-element.3) | data formatting | bytes 2097152

commit v4 on v3

--- a/solution.py
+++ b/solution.py
@@ -149,7 +149,7 @@
         loads[h, step] = pltpu.make_async_copy(a_hbm.at[rows], abuf.at[rows], load_sem.at[i])
     t_loads[0].start()
     t_loads[1].start()
-    for unit in units:
+    for unit in units[:2]:
         loads[unit].start()
     for p in range(2):
         t_loads[p].wait()
@@ -195,7 +195,8 @@
         return remote(ref, ref, ag_send.at[p, d, 2], ag_recv.at[p, d, 2], col=to(d))
 
     def sketch(h, step):
-        loads[h, step].wait()
+        if (h, step) != units[0]:
+            loads[h, step].wait()
         rows = ds(base(h, chunk(step)), CH)
         high, low = split(abuf[rows, :])
         ahi[rows, :] = high
@@ -443,29 +444,34 @@
         for d in range(2):
             gather_on(p, d).wait_recv()
 
-    for unit in units[:4]:
+    loads[units[0]].wait()
+    for unit in units[2:]:
+        loads[unit].start()
+    for unit in units[:2]:
         sketch(*unit)
     pl.semaphore_wait(barrier, (YS - 1) + (XS - 1) + (KS - 1) + (ZS - 1))
-    for make in (relay, direct):
+    for p in range(2):
         for d in range(2):
-            go(make(0, d))
-    for unit in units[4:6]:
+            go(relay(p, d))
+    for unit in units[2:4]:
         sketch(*unit)
     for d in range(2):
-        go(relay(1, d))
-    for unit in units[6:]:
+        go(direct(0, d))
+    for unit in units[4:6]:
         sketch(*unit)
     pass_on(0)
     for d in range(2):
         go(direct(1, d))
     pass_on(1)
+    for unit in units[6:]:
+        sketch(*unit)
     own_sum(0)
     for d in range(2):
         go(gather(0, d, d))
+    gram_local(0)
+    product(0, 0, 0, True)
     for d in range(2):
         go(gather(0, d, 1 - d))
-    gram_local(0)
-    product(0, 0, 0, True)
     product(0, 1, 0)
     g_core(0)
     own_sum(1)
@@ -490,28 +496,22 @@
     product(0, 0, 2)
     product(0, 1, 2)
     c_send(0)
+    gathered_first(1)
     c_core(0)
-    gathered_first(1)
     g_y(0)
     product(1, 0, 3)
     product(1, 1, 1)
-    g_z(1)
     gathered_second(1)
     product(1, 1, 3)
     product(1, 0, 1)
-    g_x_back(0)
+    g_z(1)
     c_x(0)
-    g_y(1)
-
-    @role(1)
-    def _():
-        factor_start0()
-        eliminate(work.at[0], 0)
-
     gathered_last(1)
     product(1, 0, 2)
     product(1, 1, 2)
     c_send(1)
+    g_y(1)
+    g_x_back(0)
 
     def first():
         both = dot3(split(inv[:, :128]), split(gathered(0)))
@@ -528,7 +528,8 @@
 
     @role(1)
     def _():
-        for i in (4, 8, 12):
+        factor_start0()
+        for i in (0, 4, 8, 12):
             eliminate(work.at[0], i)
 
     g_x_back(1)

time: 81.4 us -> 78.6 us (0.966)
  Pallas kernels: 78.4 us -> 75.6 us
    pallas_call x1, Pallas kernels: 78.4 us -> 75.6 us  [per_device(): pl.pallas_call(comm_kernel, out_shape=(vmem((ROWS, 256), F32), vmem((256,...]
where the time goes in v4:
time: 78.6 us; the launch traced here: 78.5 us
  Pallas kernels  75.6 us (96%)
  local copies, waits for them, and re-layouts  2.29 us (3%)
    pallas_call x1, Pallas kernels, per_device(): pl.pallas_call(comm_kernel, out_shape=(vmem((ROWS, 256), F32), vmem((256,...  75.6 us
    unnamed x2, local copies, waits for them, and re-layouts  2.29 us

profile of v4, /device:TPU:1, one launch (start us, length us, event | category | flops | bytes accessed | tf_op | source)
XLA Modules:
  0.0 78.5 jit_solution(15132156130276976332)
XLA Ops:
  0.6 75.6 %shard_map.41 = (f32[2048,256]{1,0:T(8,128)S(1)}, f32[256,1024]{1,0:T(8,128)S(1)}) custom-call(f32[2048,1024]{1,0:T(8,128)} %a_hbm.1, f32[2,1024,128]{2,1,0:T(8,128)} %t_hbm.1), custom_call_target="tpu_custom_call" | custom-call | tf_op jit(solution)/shard_map/pallas_call | solution.py:569
  76.2 1.3 %copy.6 = f32[2048,256]{1,0:T(8,128)} copy(f32[2048,256]{1,0:T(8,128)S(1)} %get-tuple-element.2) | data formatting | bytes 4194304
  77.5 1.0 %copy.7 = f32[256,1024]{1,0:T(8,128)} copy(f32[256,1024]{1,0:T(8,128)S(1)} %get-tuple-element.3) | data formatting | bytes 2097152

commit v5 on v4

--- a/solution.py
+++ b/solution.py
@@ -563,10 +563,22 @@
         copy.wait_send()
 
 
+def store_kernel(basis_ref, coeff_ref, basis_hbm, coeff_hbm, sem):
+    copies = []
+    for src, dst, count in ((basis_ref, basis_hbm, 8), (coeff_ref, coeff_hbm, 4)):
+        size = src.shape[0] // count
+        for i in range(count):
+            rows = pl.ds(i * size, size)
+            copies.append(pltpu.make_async_copy(src.at[rows], dst.at[rows], sem.at[len(copies)]))
+            copies[-1].start()
+    for copy in copies:
+        copy.wait()
+
+
 def per_device(snapshots, tests):
     vmem, dma = pltpu.VMEM, pltpu.SemaphoreType.DMA
     any_spec = pl.BlockSpec(memory_space=pl.ANY)
-    return pl.pallas_call(
+    basis, coeffs = pl.pallas_call(
         comm_kernel,
         out_shape=(vmem((ROWS, 256), F32), vmem((256, COLS), F32)),
         in_specs=[any_spec, any_spec],
@@ -585,6 +597,14 @@
             dma((2,)), dma((2,)), dma((2, 2, 3)), dma((2, 2, 3)), dma((2, 7)), dma((2, 7)), dma((2, 3)), dma((2, 3))],
         compiler_params=pltpu.CompilerParams(collective_id=0, has_side_effects=True, vmem_limit_bytes=52 << 20),
     )(snapshots, tests)
+    return pl.pallas_call(
+        store_kernel,
+        out_shape=(jax.ShapeDtypeStruct((ROWS, 256), F32), jax.ShapeDtypeStruct((256, COLS), F32)),
+        in_specs=[pl.BlockSpec(memory_space=vmem), pl.BlockSpec(memory_space=vmem)],
+        out_specs=(any_spec, any_spec),
+        scratch_shapes=[dma((12,))],
+        compiler_params=pltpu.CompilerParams(vmem_limit_bytes=8 << 20),
+    )(basis, coeffs)
 
 
 def solution(mesh):

time: 78.6 us -> 78.2 us (level)
  local copies, waits for them, and re-layouts: 2.29 us -> 0 us
  Pallas kernels: 75.6 us -> 77.3 us
    unnamed x2 -> x0, local copies, waits for them, and re-layouts: 2.29 us -> none
    pallas_call x0 -> x1, Pallas kernels: none -> 1.76 us  [per_device(): pl.pallas_call(store_kernel, out_shape=(jax.ShapeDtypeStruct((ROWS, 256),...]
where the time goes in v5:
time: 78.2 us; the launch traced here: 78.1 us
  Pallas kernels  77.3 us (99%)
  between operations  0.8 us (1%)
    pallas_call x1, Pallas kernels, per_device(): pl.pallas_call(comm_kernel, out_shape=(vmem((ROWS, 256), F32), vmem((256,...  75.6 us
    pallas_call x1, Pallas kernels, per_device(): pl.pallas_call(store_kernel, out_shape=(jax.ShapeDtypeStruct((ROWS, 256),...  1.76 us

profile of v5, /device:TPU:1, one launch (start us, length us, event | category | flops | bytes accessed | tf_op | source)
XLA Modules:
  0.0 78.1 jit_solution(16435544148163922965)
XLA Ops:
  0.6 75.6 %shard_map.41 = (f32[2048,256]{1,0:T(8,128)S(1)}, f32[256,1024]{1,0:T(8,128)S(1)}) custom-call(f32[2048,1024]{1,0:T(8,128)} %a_hbm.1, f32[2,1024,128]{2,1,0:T(8,128)} %t_hbm.1), custom_call_target="tpu_custom_call" | custom-call | tf_op jit(solution)/shard_map/pallas_call | solution.py:581
  76.2 1.8 %shard_map.42 = (f32[2048,256]{1,0:T(8,128)}, f32[256,1024]{1,0:T(8,128)}) custom-call(f32[2048,256]{1,0:T(8,128)S(1)} %get-tuple-element.4.basis_ref, f32[256,1024]{1,0:T(8,128)S(1)} %get-tuple-element.5.coeff_ref), custom_call_target="tpu_custom_call" | custom-call | tf_op jit(solution)/shard_map/pallas_call | solution.py:600
